TPU v7x, 128 devices: a whole 4x4x4 slice. The times are simulated.
128 devices in a mesh: pipe: 4 (over x_hi, core), dp: 32 (over y, z, x_lo).
Axes of the slice: x: 4 (x_hi: 2, x_lo: 2; x = x_hi * 2 + x_lo), y: 4, z: 4, core: 2. Of those that a mesh axis runs over, the one named last changes fastest.
Arguments:
- layer_input: bfloat16 [4, 4096, 8192], P('pipe', 'dp'), may hold values from -130 to 130
- queries: bfloat16 [4, 4096, 4096], P('pipe', 'dp'), may hold values from -35 to 35
- out_grad: bfloat16 [4, 4096, 4096], P('pipe', 'dp'), may hold values from -6 to 6
- top_grad: bfloat16 [4096, 8192], P('dp'), may hold values from -4 to 4
- norm_gain: bfloat16 [4, 8192], P('pipe', 'dp'), may hold values from 0.5 to 1.5
- key_weight: bfloat16 [4, 8192, 512], P('pipe', 'dp'), may hold values from -0.0625 to 0.0625
- value_weight: bfloat16 [4, 8192, 512], P('pipe', 'dp'), may hold values from -0.0625 to 0.0625
- weight_exponents: int32 [4, 2, 64, 4], P('pipe', None, 'dp'), may hold values from -1 to 1
- doc_lengths: int32 [64], replicated, may hold values from 1 to 512, 4096 in all
Outputs:
- input_grad: bfloat16 [4, 4096, 8192], P('pipe', 'dp')
- query_grad: bfloat16 [4, 4096, 4096], P('pipe', 'dp')
- key_weight_grad: float32 [4, 8192, 512], P('pipe', 'dp')
- value_weight_grad: float32 [4, 8192, 512], P('pipe', 'dp')
- gain_grad: float32 [4, 8192], P('pipe', 'dp')
Inputs may be any that keep to these rules, and one draw needn't show every extreme that they name: `doc_lengths`: the lengths sum to 4096; the longest is exactly 512. `weight_exponents`: one exponent of two for each 128 x 128 block.
All inputs are finite; a program needn't handle non-finite values.
Results may differ from a plain program's by a relative error of at most 0.035.
The roundings to bfloat16 on the way count: a program that leaves them out, or rounds other values in their place, can miss the bound.
Values may be sent and summed in bfloat16 or wider, within the bound.
A program may use at most 192 MiB of HBM per device.

v0:
```python
from functools import reduce
import math
import jax
import jax.numpy as jnp
from jax import lax
from jax.sharding import PartitionSpec as P

KV_HEADS = 4
Q_PER_KV = 8
HEAD = 128
BLOCK = 128
REACH = 4
theta_base = 500000.0
eps_norm = 1e-05
masked_score = -1e30


def passed_along(block, axis, distance):
    devices = range(lax.axis_size(axis))
    route = [(i - distance, i) for i in devices if i - distance in devices]
    return lax.ppermute(block, axis, route)


def rotary_tables(positions, head_size):
    half_size = head_size // 2
    frequency = theta_base ** (-(jnp.arange(half_size).astype(jnp.float32) * 2.0 / head_size))
    angles = positions.astype(jnp.float32)[:, None] * frequency[None, :]
    return (jnp.cos(angles)[:, None, :], jnp.sin(angles)[:, None, :])


def rotate(values, cosine, sine):
    half_size = values.shape[-1] // 2
    first = values[..., :half_size]
    second = values[..., half_size:]
    return jnp.concatenate(
        [first * cosine - second * sine, second * cosine + first * sine], axis=-1
    )


def unrotate(grads, cosine, sine):
    half_size = grads.shape[-1] // 2
    first = grads[..., :half_size]
    second = grads[..., half_size:]
    return jnp.concatenate(
        [first * cosine + second * sine, second * cosine - first * sine], axis=-1
    )


def doc_info(token_index, doc_lengths):
    starts = jnp.cumsum(doc_lengths) - doc_lengths
    before = starts[None, :] <= token_index[:, None]
    doc_number = jnp.sum(before.astype(jnp.int32), axis=1) - 1
    doc_start = jnp.max(jnp.where(before, starts[None, :], 0), axis=1)
    return (doc_number, token_index - doc_start)


def dequantize(values, exponents, block_side):
    row_blocks, col_blocks = exponents.shape
    factors = jnp.exp2(exponents.astype(jnp.float32))
    shaped = values.astype(jnp.float32).reshape(row_blocks, block_side, col_blocks, block_side)
    return (shaped * factors[:, None, :, None]).reshape(values.shape).astype(jnp.bfloat16)


def guarded(compute):
    result = compute()
    return result


def on_device(
    layer_input,
    queries,
    out_grad,
    top_grad,
    norm_gain,
    key_weight,
    value_weight,
    weight_exponents,
    doc_lengths,
):
    local_rows = layer_input.shape[1]
    kv_heads = KV_HEADS
    group_size = Q_PER_KV
    head_size = HEAD
    dp_index = lax.axis_index("dp")
    section_index = lax.axis_index("pipe")
    sections = lax.axis_size("pipe")
    key_local = dequantize(key_weight[0], weight_exponents[0, 0], BLOCK)
    value_local = dequantize(value_weight[0], weight_exponents[0, 1], BLOCK)
    key_full, value_full, gain_full = (
        lax.all_gather(key_local, "dp", axis=0, tiled=True),
        lax.all_gather(value_local, "dp", axis=0, tiled=True),
        lax.all_gather(norm_gain[0], "dp", axis=0, tiled=True),
    )
    inputs = layer_input[0].astype(jnp.float32)
    root_mean = jnp.sqrt(jnp.mean(inputs * inputs, axis=1, keepdims=True) + eps_norm)
    normed = inputs / root_mean
    gain_f = gain_full.astype(jnp.float32)
    hidden = (normed * gain_f).astype(jnp.bfloat16)
    token_index = dp_index * local_rows + jnp.arange(local_rows)
    query_doc, query_pos = doc_info(token_index, doc_lengths)
    cosine, sine = rotary_tables(query_pos, head_size)
    key_proj = jnp.dot(hidden, key_full, preferred_element_type=jnp.float32).reshape(
        local_rows, kv_heads, head_size
    )
    keys_own = rotate(key_proj, cosine, sine).astype(jnp.bfloat16)
    values_own = (
        jnp.dot(hidden, value_full, preferred_element_type=jnp.float32)
        .astype(jnp.bfloat16)
        .reshape(local_rows, kv_heads, head_size)
    )
    key_blocks = [None] * (REACH + 1)
    value_blocks = [None] * (REACH + 1)
    key_blocks[REACH] = keys_own
    value_blocks[REACH] = values_own
    own_pair = jnp.stack((keys_own, values_own))
    for distance in range(1, REACH + 1):
        got_pair = passed_along(own_pair, "dp", distance)
        key_blocks[REACH - distance] = got_pair[0]
        value_blocks[REACH - distance] = got_pair[1]
    inv_root = 1.0 / math.sqrt(head_size)
    query_groups = queries[0].reshape(local_rows, kv_heads, group_size, head_size)
    grad_groups = out_grad[0].reshape(local_rows, kv_heads, group_size, head_size)
    visibility = []
    seen_flags = []
    for block_number in range(REACH + 1):
        key_index = (dp_index - REACH + block_number) * local_rows + jnp.arange(local_rows)
        key_doc, unused = doc_info(key_index, doc_lengths)
        visible = (
            (key_index[None, :] >= 0)
            & (key_doc[None, :] == query_doc[:, None])
            & (key_index[None, :] <= token_index[:, None])
        )
        visibility.append(visible)
        seen_flags.append(jnp.any(visible))

    def score_block(block_number):

        def compute():
            raw_scores = jnp.einsum(
                "qkgd,tkd->kgqt",
                query_groups,
                key_blocks[block_number],
                preferred_element_type=jnp.float32,
            )
            return jnp.where(
                visibility[block_number][None, None], raw_scores * inv_root, masked_score
            )

        return guarded(compute)

    scores = [score_block(block_number) for block_number in range(REACH + 1)]
    row_max = reduce(jnp.maximum, [jnp.max(member, axis=3, keepdims=True) for member in scores])
    exp_scores = [jnp.exp(member - row_max) for member in scores]
    row_total = reduce(jnp.add, [jnp.sum(member, axis=3, keepdims=True) for member in exp_scores])
    softmax_out = [member / row_total for member in exp_scores]
    probs_low = [member.astype(jnp.bfloat16) for member in softmax_out]

    def attend_block(block_number):

        def compute():
            return jnp.einsum(
                "kgqt,tkd->qkgd",
                probs_low[block_number],
                value_blocks[block_number],
                preferred_element_type=jnp.float32,
            )

        return guarded(compute)

    attended = reduce(jnp.add, [attend_block(block_number) for block_number in range(REACH + 1)])
    out_dot = jnp.transpose(jnp.sum(grad_groups.astype(jnp.float32) * attended, axis=3), (1, 2, 0))[
        ..., None
    ]

    def grads_block(block_number):

        def compute():
            value_term = jnp.einsum(
                "kgqt,qkgd->tkd",
                probs_low[block_number],
                grad_groups,
                preferred_element_type=jnp.float32,
            )
            prob_grad = jnp.einsum(
                "qkgd,tkd->kgqt",
                grad_groups,
                value_blocks[block_number],
                preferred_element_type=jnp.float32,
            )
            score_grads = (softmax_out[block_number] * (prob_grad - out_dot)).astype(jnp.bfloat16)
            query_term = jnp.einsum(
                "kgqt,tkd->qkgd",
                score_grads,
                key_blocks[block_number],
                preferred_element_type=jnp.float32,
            )
            key_term = (
                jnp.einsum(
                    "kgqt,qkgd->tkd", score_grads, query_groups, preferred_element_type=jnp.float32
                )
                * inv_root
            )
            return (query_term, key_term.astype(jnp.bfloat16), value_term.astype(jnp.bfloat16))

        return guarded(compute)

    block_grads = [grads_block(block_number) for block_number in range(REACH + 1)]
    query_grad = (
        (reduce(jnp.add, [member[0] for member in block_grads]) * inv_root)
        .astype(jnp.bfloat16)
        .reshape(1, local_rows, -1)
    )
    key_sum = block_grads[REACH][1].astype(jnp.float32)
    value_sum = block_grads[REACH][2].astype(jnp.float32)
    for distance in range(1, REACH + 1):
        sent_pair = jnp.stack((block_grads[REACH - distance][1], block_grads[REACH - distance][2]))
        back_pair = passed_along(sent_pair, "dp", -distance)
        key_sum = key_sum + back_pair[0].astype(jnp.float32)
        value_sum = value_sum + back_pair[1].astype(jnp.float32)
    key_grads = unrotate(key_sum, cosine, sine).astype(jnp.bfloat16).reshape(local_rows, -1)
    value_grads = value_sum.astype(jnp.bfloat16).reshape(local_rows, -1)
    hidden_grad = jnp.einsum(
        "tc,dc->td", key_grads, key_full, preferred_element_type=jnp.float32
    ) + jnp.einsum("tc,dc->td", value_grads, value_full, preferred_element_type=jnp.float32)
    gain_term = jnp.sum(hidden_grad * normed, axis=0)
    scaled_grad = hidden_grad * gain_f
    branch = (
        scaled_grad - normed * jnp.mean(scaled_grad * normed, axis=1, keepdims=True)
    ) / root_mean
    last_section = sections - 1
    carried = jnp.where(
        section_index == last_section,
        (top_grad.astype(jnp.float32) + branch).astype(jnp.bfloat16),
        jnp.zeros_like(top_grad),
    )
    for step_number in range(sections - 1):
        received = passed_along(carried, "pipe", -1)
        carried = jnp.where(
            section_index == last_section - 1 - step_number,
            (received.astype(jnp.float32) + branch).astype(jnp.bfloat16),
            carried,
        )
    key_full_grad = jnp.einsum("tr,tc->rc", hidden, key_grads, preferred_element_type=jnp.float32)
    value_full_grad = jnp.einsum(
        "tr,tc->rc", hidden, value_grads, preferred_element_type=jnp.float32
    )
    key_wgrad, value_wgrad, gain_grad = (
        lax.psum_scatter(
            key_full_grad.astype(jnp.bfloat16), "dp", scatter_dimension=0, tiled=True
        ).astype(jnp.float32),
        lax.psum_scatter(
            value_full_grad.astype(jnp.bfloat16), "dp", scatter_dimension=0, tiled=True
        ).astype(jnp.float32),
        lax.psum_scatter(
            gain_term.astype(jnp.bfloat16), "dp", scatter_dimension=0, tiled=True
        ).astype(jnp.float32),
    )
    return (carried[None], query_grad, key_wgrad[None], value_wgrad[None], gain_grad[None])


def solution(mesh):
    in_specs = (
        P("pipe", "dp", None),
        P("pipe", "dp", None),
        P("pipe", "dp", None),
        P("dp", None),
        P("pipe", "dp"),
        P("pipe", "dp", None),
        P("pipe", "dp", None),
        P("pipe", None, "dp", None),
        P(),
    )
    out_specs = (
        P("pipe", "dp", None),
        P("pipe", "dp", None),
        P("pipe", "dp", None),
        P("pipe", "dp", None),
        P("pipe", "dp"),
    )
    return jax.shard_map(
        on_device, mesh=mesh, in_specs=in_specs, out_specs=out_specs, check_vma=False
    )
```

profile of v0, /device:TPU:0, one launch (start us, length us, event | category | flops | bytes accessed | tf_op | source)
XLA Modules:
  0.0 965.6 jit_solution(9609781831915114517)
XLA Ops:
  8.2 1.7 fusion.70
  11.0 82.9 %all-gather = bf16[1,8192]{1,0:T(2,128)(2,1)S(1)} all-gather(bf16[1,256]{1,0:T(2,128)(2,1)S(1)} %copy-done.38), channel_id=2, replica_groups=mesh['pipe'=4,'dp'=32] {'dp'}, dimensions={1}, use_global_device_ids=true | all-gather | bytes 16896 | tf_op jit(solution)/shard_map/all_gather | solution.py:92
  95.5 2.1 fusion.2
  98.8 104.8 %all-gather.6.cloned.1.call-done = bf16[8192,512]{1,0:T(8,128)(2,1)} async-done(((bf16[256,512]{1,0:T(8,128)(2,1)}), bf16[8192,512]{1,0:T(8,128)(2,1)}) %all-gather.6.cloned.1.call-update) | async-done | bytes 8388624 | tf_op jit(solution)/shard_map/all_gather | solution.py:91
  203.7 5.3 fusion.49
  209.2 184.8 %all-gather.4.cloned.1.call-done = bf16[8192,512]{1,0:T(8,128)(2,1)} async-done(((bf16[256,512]{1,0:T(8,128)(2,1)}), bf16[8192,512]{1,0:T(8,128)(2,1)}) %all-gather.4.cloned.1.call-update) | async-done | bytes 8388624 | tf_op jit(solution)/shard_map/all_gather | solution.py:90
  393.9 12.0 %copy.180 = bf16[512,8192]{1,0:T(8,128)(2,1)} copy(bf16[512,8192]{0,1:T(8,128)(2,1)} %bitcast.450) | data formatting | bytes 16777216 | tf_op jit(solution)/shard_map/dot_general | solution.py:102
  406.0 6.4 fusion.22
  414.5 1.5 collective-permute-start.2
  416.0 4.1 collective-permute-start.1
  420.1 5.4 collective-permute-start
  427.1 9.1 collective-permute-done
  439.0 3.3 fusion.32
  442.3 2.4 fusion.65
  461.1 4.6 collective-permute-done.4
  465.7 7.0 collective-permute-done.5
  475.1 5.7 convolution_convert_fusion
  481.0 2.4 fusion.21
  485.5 5.7 convolution_convert_fusion.1
  491.2 6.4 fusion.106
  497.6 6.0 multiply_reduce_fusion
  503.7 2.8 fusion.6
  507.8 4.9 collective-permute-done.8
  512.7 4.9 fusion.7
  519.1 71.2 %collective-permute-done.9 = bf16[128,8192]{1,0:T(8,128)(2,1)} collective-permute-done((bf16[128,8192]{1,0:T(8,128)(2,1)}, bf16[128,8192]{1,0:T(8,128)(2,1)}, u32[]{:S(2)}, u32[]{:S(2)}) %collective-permute-start.9) | collective-permute-done | bytes 2097184 | tf_op jit(solution)/shard_map/ppermute | solution.py:21
  590.3 6.0 fusion.8
  599.5 1.7 fusion.81
  606.8 171.8 %all-reduce = bf16[8192]{0:T(1024)(128)(2,1)S(1)} all-reduce(bf16[8192]{0:T(1024)(128)(2,1)S(1)} %get-tuple-element.25), channel_id=5, replica_groups=mesh['pipe'=4,'dp'=32] {'dp'}, use_global_device_ids=true, to_apply=%region_23.24.clone | all-reduce | flops 8192 | bytes 32768
  779.3 7.0 fusion.10
  786.3 1.8 bitcast_convert_fusion
  788.1 168.9 %reduce-scatter.3.cloned.1.call-done = bf16[256,512]{1,0:T(8,128)(2,1)} async-done(((bf16[8192,512]{1,0:T(8,128)(2,1)}), bf16[256,512]{1,0:T(8,128)(2,1)}) %reduce-scatter.3.cloned.1.call-update) | async-done | bytes 262160 | tf_op jit(solution)/shard_map/reduce_scatter | solution.py:248
  957.0 1.8 bitcast_convert_fusion.1
  (203 shorter events, 43.1 us)
Async XLA Ops:
  7.2 86.8 %copy-start.43 = (s32[64]{0:T(128)S(1)}, s32[64]{0:T(128)}, u32[]{:S(2)}) copy-start(s32[64]{0:T(128)} %param.17) | copy-start | bytes 772
  7.2 87.1 %copy-start.10 = (bf16[1,128,4096]{2,1,0:T(8,128)(2,1)S(1)}, bf16[1,128,4096]{2,1,0:T(8,128)(2,1)}, u32[]{:S(2)}) copy-start(bf16[1,128,4096]{2,1,0:T(8,128)(2,1)} %param.10) | copy-start | bytes 3145732
  7.2 196.4 %all-gather.6.cloned.1.call-start = ((), (), s32[]{:S(2)}) async-start(), calls=%async_computation.3 | async-start | bytes 8650752 | tf_op jit(solution)/shard_map/all_gather | solution.py:91
  9.9 384.0 %all-gather.4.cloned.1.call-start = ((), (), s32[]{:S(2)}) async-start(), calls=%async_computation.2 | async-start | bytes 8650752 | tf_op jit(solution)/shard_map/all_gather | solution.py:90
  10.0 84.6 %copy-start.11 = (bf16[1,128,4096]{2,1,0:T(8,128)(2,1)S(1)}, bf16[1,128,4096]{2,1,0:T(8,128)(2,1)}, u32[]{:S(2)}) copy-start(bf16[1,128,4096]{2,1,0:T(8,128)(2,1)} %param.11) | copy-start | bytes 3145732
  11.0 775.3 %reduce-scatter.5.cloned.1.call-start = ((), (), s32[]{:S(2)}) async-start(), calls=%async_computation.5 | async-start | bytes 8650752 | tf_op jit(solution)/shard_map/reduce_scatter | solution.py:251
  94.0 312.0 %copy-start.29 = (f32[1,8192]{1,0:T(1,128)}, f32[1,8192]{1,0:T(1,128)S(1)}, u32[]{:S(2)}) copy-start(f32[1,8192]{1,0:T(1,128)S(1)} %convert_element_type.409) | copy-start | bytes 98308
  97.6 308.4 %copy-start.39 = (f32[128]{0:T(128)}, f32[128]{0:T(128)S(1)}, u32[]{:S(2)}) copy-start(f32[128]{0:T(128)S(1)} %add_sqrt_fusion) | copy-start | bytes 1540
  97.9 314.5 %copy-start.24 = (f32[128,64]{0,1:T(8,128)}, f32[128,64]{0,1:T(8,128)S(1)}, u32[]{:S(2)}) copy-start(f32[128,64]{0,1:T(8,128)S(1)} %get-tuple-element.56) | copy-start | bytes 98308
  97.9 314.5 %copy-start.26 = (f32[128,64]{0,1:T(8,128)}, f32[128,64]{0,1:T(8,128)S(1)}, u32[]{:S(2)}) copy-start(f32[128,64]{0,1:T(8,128)S(1)} %get-tuple-element.57) | copy-start | bytes 98308
  413.2 25.1 %collective-permute-start.3 = (bf16[2,128,4,128]{1,3,2,0:T(8,128)(2,1)}, bf16[2,128,4,128]{1,3,2,0:T(8,128)(2,1)S(1)}, u32[]{:S(2)}, u32[]{:S(2)}) collective-permute-start(bf16[2,128,4,128]{1,3,2,0:T(8,128)(2,1)} %pad_maximum_fusion), channel_id=1, source_target_pairs={{0,1},{1,2},{2,3},{3,4},{4,5},{5,6},{6,7},{7,8},{8,9},{9,10},{10,1... | collective-permute-start | bytes 786440 | tf_op jit(solution)/shard_map/ppermute | solution.py:21
  414.5 23.1 %collective-permute-start.2 = (bf16[2,128,4,128]{1,3,2,0:T(8,128)(2,1)}, bf16[2,128,4,128]{1,3,2,0:T(8,128)(2,1)S(1)}, u32[]{:S(2)}, u32[]{:S(2)}) collective-permute-start(bf16[2,128,4,128]{1,3,2,0:T(8,128)(2,1)} %pad_maximum_fusion), channel_id=1, source_target_pairs={{0,2},{1,3},{2,4},{3,5},{4,6},{5,7},{6,8},{7,9},{8,10},{9,11},{10,... | collective-permute-start | bytes 786440 | tf_op jit(solution)/shard_map/ppermute | solution.py:21
  416.0 20.9 %collective-permute-start.1 = (bf16[2,128,4,128]{1,3,2,0:T(8,128)(2,1)}, bf16[2,128,4,128]{1,3,2,0:T(8,128)(2,1)S(1)}, u32[]{:S(2)}, u32[]{:S(2)}) collective-permute-start(bf16[2,128,4,128]{1,3,2,0:T(8,128)(2,1)} %pad_maximum_fusion), channel_id=1, source_target_pairs={{0,3},{1,4},{2,5},{3,6},{4,7},{5,8},{6,9},{7,10},{8,11},{9,12},{10... | collective-permute-start | bytes 786440 | tf_op jit(solution)/shard_map/ppermute | solution.py:21
  420.1 16.1 %collective-permute-start = (bf16[2,128,4,128]{1,3,2,0:T(8,128)(2,1)}, bf16[2,128,4,128]{1,3,2,0:T(8,128)(2,1)S(1)}, u32[]{:S(2)}, u32[]{:S(2)}) collective-permute-start(bf16[2,128,4,128]{1,3,2,0:T(8,128)(2,1)} %pad_maximum_fusion), channel_id=1, source_target_pairs={{0,4},{1,5},{2,6},{3,7},{4,8},{5,9},{6,10},{7,11},{8,12},{9,13},{1... | collective-permute-start | bytes 786440 | tf_op jit(solution)/shard_map/ppermute | solution.py:21
  425.6 20.9 %copy-start.23 = (bf16[128,4,128,1]{0,2,3,1:T(8,128)(2,1)}, bf16[128,4,128,1]{0,2,3,1:T(8,128)(2,1)S(1)}, u32[]{:S(2)}) copy-start(bf16[128,4,128,1]{0,2,3,1:T(8,128)(2,1)S(1)} %copy.249) | copy-start | bytes 393220
  425.6 10.6 %copy-start.35 = (pred[128,128]{0,1:T(8,128)(4,1)S(1)}, pred[128,128]{0,1:T(8,128)(4,1)}, u32[]{:S(2)}) copy-start(pred[128,128]{0,1:T(8,128)(4,1)} %get-tuple-element.51) | copy-start | bytes 49156
  427.1 15.2 %copy-start = (f32[4,8,128,128]{2,3,1,0:T(8,128)}, f32[4,8,128,128]{2,3,1,0:T(8,128)S(1)}, u32[]{:S(2)}) copy-start(f32[4,8,128,128]{2,3,1,0:T(8,128)S(1)} %get-tuple-element.59) | copy-start | bytes 6291460
  436.2 11.6 %copy-start.17 = (bf16[2,128,4,128]{1,3,2,0:T(8,128)(2,1)}, bf16[2,128,4,128]{1,3,2,0:T(8,128)(2,1)S(1)}, u32[]{:S(2)}) copy-start(bf16[2,128,4,128]{1,3,2,0:T(8,128)(2,1)S(1)} %collective-permute-done) | copy-start | bytes 786436
  436.9 10.5 %copy-start.14 = (bf16[2,128,4,128]{1,3,2,0:T(8,128)(2,1)}, bf16[2,128,4,128]{1,3,2,0:T(8,128)(2,1)S(1)}, u32[]{:S(2)}) copy-start(bf16[2,128,4,128]{1,3,2,0:T(8,128)(2,1)S(1)} %collective-permute-done.1) | copy-start | bytes 786436
  438.3 9.9 %copy-start.20 = (bf16[2,128,4,128]{1,3,2,0:T(8,128)(2,1)}, bf16[2,128,4,128]{1,3,2,0:T(8,128)(2,1)S(1)}, u32[]{:S(2)}) copy-start(bf16[2,128,4,128]{1,3,2,0:T(8,128)(2,1)S(1)} %collective-permute-done.3) | copy-start | bytes 786436
  442.3 11.3 %copy-start.36 = (f32[4,8,128]{2,1,0:T(8,128)}, f32[4,8,128]{2,1,0:T(8,128)S(1)}, u32[]{:S(2)}) copy-start(f32[4,8,128]{2,1,0:T(8,128)S(1)} %add_add_fusion) | copy-start | bytes 49156
  455.4 19.7 %copy-start.1 = (bf16[1,128,8192]{2,1,0:T(8,128)(2,1)S(1)}, bf16[1,128,8192]{2,1,0:T(8,128)(2,1)}, u32[]{:S(2)}) copy-start(bf16[1,128,8192]{2,1,0:T(8,128)(2,1)} %param.9) | copy-start | bytes 6291460
  455.5 19.7 %copy-start.30 = (f32[1,8192]{1,0:T(1,128)S(1)}, f32[1,8192]{1,0:T(1,128)}, u32[]{:S(2)}) copy-start(f32[1,8192]{1,0:T(1,128)} %copy-done.29) | copy-start | bytes 98308
  455.5 19.7 %copy-start.40 = (f32[128]{0:T(128)S(1)}, f32[128]{0:T(128)}, u32[]{:S(2)}) copy-start(f32[128]{0:T(128)} %copy-done.39) | copy-start | bytes 1540
  455.5 10.2 %collective-permute-start.4 = (bf16[2,128,4,128]{1,3,2,0:T(8,128)(2,1)S(1)}, bf16[2,128,4,128]{1,3,2,0:T(8,128)(2,1)S(1)}, u32[]{:S(2)}, u32[]{:S(2)}) collective-permute-start(bf16[2,128,4,128]{1,3,2,0:T(8,128)(2,1)S(1)} %pad_maximum_fusion.1), channel_id=1, source_target_pairs={{1,0},{2,1},{3,2},{4,3},{5,4},{6,5},{7,6},{8,7},{9,8},{10,9},{11,1... | collective-permute-start | bytes 786440 | tf_op jit(solution)/shard_map/ppermute | solution.py:21
  456.9 15.7 %collective-permute-start.5 = (bf16[2,128,4,128]{1,3,2,0:T(8,128)(2,1)S(1)}, bf16[2,128,4,128]{1,3,2,0:T(8,128)(2,1)S(1)}, u32[]{:S(2)}, u32[]{:S(2)}) collective-permute-start(bf16[2,128,4,128]{1,3,2,0:T(8,128)(2,1)S(1)} %pad_maximum_fusion.2), channel_id=1, source_target_pairs={{2,0},{3,1},{4,2},{5,3},{6,4},{7,5},{8,6},{9,7},{10,8},{11,9},{12,... | collective-permute-start | bytes 786440 | tf_op jit(solution)/shard_map/ppermute | solution.py:21
  458.3 14.4 %collective-permute-start.6 = (bf16[2,128,4,128]{1,3,2,0:T(8,128)(2,1)S(1)}, bf16[2,128,4,128]{1,3,2,0:T(8,128)(2,1)S(1)}, u32[]{:S(2)}, u32[]{:S(2)}) collective-permute-start(bf16[2,128,4,128]{1,3,2,0:T(8,128)(2,1)S(1)} %pad_maximum_fusion.3), channel_id=1, source_target_pairs={{3,0},{4,1},{5,2},{6,3},{7,4},{8,5},{9,6},{10,7},{11,8},{12,9},{13... | collective-permute-start | bytes 786440 | tf_op jit(solution)/shard_map/ppermute | solution.py:21
  459.6 14.1 %collective-permute-start.7 = (bf16[2,128,4,128]{1,3,2,0:T(8,128)(2,1)S(1)}, bf16[2,128,4,128]{1,3,2,0:T(8,128)(2,1)S(1)}, u32[]{:S(2)}, u32[]{:S(2)}) collective-permute-start(bf16[2,128,4,128]{1,3,2,0:T(8,128)(2,1)S(1)} %pad_maximum_fusion.4), channel_id=1, source_target_pairs={{4,0},{5,1},{6,2},{7,3},{8,4},{9,5},{10,6},{11,7},{12,8},{13,9},{1... | collective-permute-start | bytes 786440 | tf_op jit(solution)/shard_map/ppermute | solution.py:21
  480.9 476.2 %reduce-scatter.3.cloned.1.call-start = ((), (), s32[]{:S(2)}) async-start(), calls=%async_computation.4 | async-start | bytes 8650752 | tf_op jit(solution)/shard_map/reduce_scatter | solution.py:248
  506.5 6.2 collective-permute-start.8
  517.6 72.7 %collective-permute-start.9 = (bf16[128,8192]{1,0:T(8,128)(2,1)}, bf16[128,8192]{1,0:T(8,128)(2,1)}, u32[]{:S(2)}, u32[]{:S(2)}) collective-permute-start(bf16[128,8192]{1,0:T(8,128)(2,1)} %fusion.7), channel_id=1, source_target_pairs={{32,0},{64,32},{96,64},{33,1},{65,33},{97,65},{34,2},{66,34},{98,6... | collective-permute-start | bytes 6291464 | tf_op jit(solution)/shard_map/ppermute | solution.py:21
  596.3 183.0 %collective-permute-start.10 = (bf16[128,8192]{1,0:T(8,128)(2,1)}, bf16[128,8192]{1,0:T(8,128)(2,1)}, u32[]{:S(2)}, u32[]{:S(2)}) collective-permute-start(bf16[128,8192]{1,0:T(8,128)(2,1)} %fusion.8), channel_id=1, source_target_pairs={{32,0},{64,32},{96,64},{33,1},{65,33},{97,65},{34,2},{66,34},{98,6... | collective-permute-start | bytes 6291464 | tf_op jit(solution)/shard_map/ppermute | solution.py:21
  (37 other events, 103.3 us)
Sparse Core Ops, SparseCore 0:
  10.3 193.3 all-gather.5
  205.9 187.9 all-gather.3
  481.0 214.5 reduce-scatter.4
  697.9 259.1 reduce-scatter.2
where the time goes:
time: 972 us; the launch traced here: 966 us
  waiting for transfers between devices  556 us (57%)
  blocking collectives  255 us (26%)
  matrix products  56.6 us (6%)
  other arithmetic  38.6 us (4%)
  starting transfers between devices  21.9 us (2%)
  local copies, waits for them, and re-layouts  21.4 us (2%)
  between operations  15.9 us (2%)
    all_gather x1, waiting for transfers between devices, on_device(): lax.all_gather(key_local, 'dp', axis=0, tiled=True)  185 us
    unnamed x1, blocking collectives  172 us
    reduce_scatter x1, waiting for transfers between devices, on_device(): lax.psum_scatter(key_full_grad.astype(jnp.bfloat16), 'dp', scatter_dimens...  169 us
    all_gather x1, waiting for transfers between devices, on_device(): lax.all_gather(value_local, 'dp', axis=0, tiled=True)  105 us
    ppermute x11, waiting for transfers between devices, passed_along(): return lax.ppermute(block, axis, route)  97.8 us
    all_gather x1, blocking collectives, on_device(): lax.all_gather(norm_gain[0], 'dp', axis=0, tiled=True)  82.9 us
    ppermute x11, starting transfers between devices, passed_along(): return lax.ppermute(block, axis, route)  21.8 us
  transfers between devices with their start and end apart: 15, of which 9 were waited for; matrix products, arithmetic and copies ran while one was open for 7% of the time, Pallas kernels for 0%

commit v1 on v0

--- a/solution.py
+++ b/solution.py
@@ -88,7 +88,9 @@
     value_local = dequantize(value_weight[0], weight_exponents[0, 1], BLOCK)
     key_full, value_full, gain_full = (
         lax.all_gather(key_local, "dp", axis=0, tiled=True),
-        lax.all_gather(value_local, "dp", axis=0, tiled=True),
+        jnp.concatenate(
+            lax.all_to_all(jnp.stack([value_local] * lax.axis_size("dp")), "dp", 0, 0), axis=0
+        ),
         lax.all_gather(norm_gain[0], "dp", axis=0, tiled=True),
     )
     inputs = layer_input[0].astype(jnp.float32)

time: 972 us -> 899 us (0.925)
  waiting for transfers between devices: 556 us -> 274 us
  blocking collectives: 255 us -> 454 us
  starting transfers between devices: 21.9 us -> 31.8 us
    all_gather x1, blocking collectives: 82.9 us -> 282 us  [on_device(): lax.all_gather(norm_gain[0], 'dp', axis=0, tiled=True)]
    all_gather x1, waiting for transfers between devices: 185 us -> 9.38 us  [on_device(): lax.all_gather(key_local, 'dp', axis=0, tiled=True)]
    all_gather x1 -> x0, waiting for transfers between devices: 105 us -> none  [on_device(): lax.all_gather(value_local, 'dp', axis=0, tiled=True)]
  transfers between devices with their start and end apart: 15 -> 15, of which waited for: 9 -> 7; matrix products, arithmetic and copies ran while one was open for 7% -> 8% of each run, Pallas kernels for 0% -> 0%
where the time goes in v1:
time: 899 us; the launch traced here: 892 us
  blocking collectives  454 us (51%)
  waiting for transfers between devices  274 us (30%)
  matrix products  55.9 us (6%)
  other arithmetic  36.5 us (4%)
  starting transfers between devices  31.8 us (4%)
  local copies, waits for them, and re-layouts  24.2 us (3%)
  between operations  15.8 us (2%)
    all_gather x1, blocking collectives, on_device(): lax.all_gather(norm_gain[0], 'dp', axis=0, tiled=True)  282 us
    unnamed x1, blocking collectives  172 us
    reduce_scatter x1, waiting for transfers between devices, on_device(): lax.psum_scatter(key_full_grad.astype(jnp.bfloat16), 'dp', scatter_dimens...  167 us
    ppermute x11, waiting for transfers between devices, passed_along(): return lax.ppermute(block, axis, route)  97.5 us
    ppermute x11, starting transfers between devices, passed_along(): return lax.ppermute(block, axis, route)  22.1 us
  transfers between devices with their start and end apart: 15, of which 7 were waited for; matrix products, arithmetic and copies ran while one was open for 8% of the time, Pallas kernels for 0%

profile of v1, /device:TPU:0, one launch (start us, length us, event | category | flops | bytes accessed | tf_op | source)
XLA Modules:
  0.0 892.4 jit_solution(11189655893695172834)
XLA Ops:
  8.1 1.7 fusion.72
  10.3 4.2 stack.31
  14.5 9.6 %all-to-all-start = ((bf16[32,256,512]{2,1,0:T(8,128)(2,1)}), bf16[32,256,512]{2,1,0:T(8,128)(2,1)}, u32[]{:S(2)}, u32[]{:S(2)}) async-start(bf16[32,256,512]{2,1,0:T(8,128)(2,1)} %stack.31), calls=%async_computation | async-start | bytes 16777216 | tf_op jit(solution)/shard_map/all_to_all | solution.py:92
  24.2 281.6 %all-gather = bf16[1,8192]{1,0:T(2,128)(2,1)S(1)} all-gather(bf16[1,256]{1,0:T(2,128)(2,1)S(1)} %copy-done.32), channel_id=2, replica_groups=mesh['pipe'=4,'dp'=32] {'dp'}, dimensions={1}, use_global_device_ids=true | all-gather | bytes 16896 | tf_op jit(solution)/shard_map/all_gather | solution.py:94
  307.3 2.1 fusion.2
  310.0 5.4 fusion.56
  315.7 9.4 %all-gather.3.cloned.1.call-done = bf16[8192,512]{1,0:T(8,128)(2,1)} async-done(((bf16[256,512]{1,0:T(8,128)(2,1)}), bf16[8192,512]{1,0:T(8,128)(2,1)}) %all-gather.3.cloned.1.call-update) | async-done | bytes 8388624 | tf_op jit(solution)/shard_map/all_gather | solution.py:90
  325.1 11.5 %copy.180 = bf16[512,8192]{1,0:T(8,128)(2,1)} copy(bf16[512,8192]{0,1:T(8,128)(2,1)} %bitcast.445) | data formatting | bytes 16777216 | tf_op jit(solution)/shard_map/dot_general | solution.py:104
  336.6 6.4 fusion.21
  347.1 8.6 collective-permute-start
  356.4 7.8 collective-permute-done
  367.0 3.3 fusion.32
  370.3 2.4 fusion.67
  388.3 4.6 collective-permute-done.4
  392.9 9.4 %collective-permute-done.5 = bf16[2,128,4,128]{1,3,2,0:T(8,128)(2,1)S(1)} collective-permute-done((bf16[2,128,4,128]{1,3,2,0:T(8,128)(2,1)S(1)}, bf16[2,128,4,128]{1,3,2,0:T(8,128)(2,1)S(1)}, u32[]{:S(2)}, u32[]{:S(2)}) %collective-permute-start.5) | collective-permute-done | bytes 262176 | tf_op jit(solution)/shard_map/ppermute | solution.py:21
  403.5 5.7 convolution_convert_fusion
  409.3 2.4 fusion.20
  413.8 5.7 convolution_convert_fusion.1
  419.5 6.4 fusion.108
  425.9 6.0 multiply_reduce_fusion
  432.0 2.8 fusion.5
  436.1 4.9 collective-permute-done.8
  441.0 4.9 fusion.6
  445.9 1.5 collective-permute-start.9
  447.4 70.7 %collective-permute-done.9 = bf16[128,8192]{1,0:T(8,128)(2,1)} collective-permute-done((bf16[128,8192]{1,0:T(8,128)(2,1)}, bf16[128,8192]{1,0:T(8,128)(2,1)}, u32[]{:S(2)}, u32[]{:S(2)}) %collective-permute-start.9) | collective-permute-done | bytes 2097184 | tf_op jit(solution)/shard_map/ppermute | solution.py:21
  518.2 6.0 fusion.7
  527.4 1.7 fusion.83
  534.7 172.4 %all-reduce = bf16[8192]{0:T(1024)(128)(2,1)S(1)} all-reduce(bf16[8192]{0:T(1024)(128)(2,1)S(1)} %get-tuple-element.25), channel_id=5, replica_groups=mesh['pipe'=4,'dp'=32] {'dp'}, use_global_device_ids=true, to_apply=%region_23.24.clone | all-reduce | flops 8192 | bytes 32768
  707.7 7.0 fusion.9
  714.7 1.8 bitcast_convert_fusion
  716.5 167.3 %reduce-scatter.3.cloned.1.call-done = bf16[256,512]{1,0:T(8,128)(2,1)} async-done(((bf16[8192,512]{1,0:T(8,128)(2,1)}), bf16[256,512]{1,0:T(8,128)(2,1)}) %reduce-scatter.3.cloned.1.call-update) | async-done | bytes 262160 | tf_op jit(solution)/shard_map/reduce_scatter | solution.py:250
  883.8 1.8 bitcast_convert_fusion.1
  (192 shorter events, 39.5 us)
Async XLA Ops:
  7.2 317.9 %all-gather.3.cloned.1.call-start = ((), (), s32[]{:S(2)}) async-start(), calls=%async_computation.3 | async-start | bytes 8650752 | tf_op jit(solution)/shard_map/all_gather | solution.py:90
  14.5 291.4 %copy-start.37 = (s32[64]{0:T(128)S(1)}, s32[64]{0:T(128)}, u32[]{:S(2)}) copy-start(s32[64]{0:T(128)} %param.17) | copy-start | bytes 772
  14.5 291.7 %copy-start.10 = (bf16[1,128,4096]{2,1,0:T(8,128)(2,1)S(1)}, bf16[1,128,4096]{2,1,0:T(8,128)(2,1)}, u32[]{:S(2)}) copy-start(bf16[1,128,4096]{2,1,0:T(8,128)(2,1)} %param.10) | copy-start | bytes 3145732
  14.5 295.6 %all-to-all-start = ((bf16[32,256,512]{2,1,0:T(8,128)(2,1)}), bf16[32,256,512]{2,1,0:T(8,128)(2,1)}, u32[]{:S(2)}, u32[]{:S(2)}) async-start(bf16[32,256,512]{2,1,0:T(8,128)(2,1)} %stack.31), calls=%async_computation | async-start | bytes 16777216 | tf_op jit(solution)/shard_map/all_to_all | solution.py:92
  24.1 282.3 %copy-start.11 = (bf16[1,128,4096]{2,1,0:T(8,128)(2,1)S(1)}, bf16[1,128,4096]{2,1,0:T(8,128)(2,1)}, u32[]{:S(2)}) copy-start(bf16[1,128,4096]{2,1,0:T(8,128)(2,1)} %param.11) | copy-start | bytes 3145732
  24.1 690.6 %reduce-scatter.5.cloned.1.call-start = ((), (), s32[]{:S(2)}) async-start(), calls=%async_computation.5 | async-start | bytes 8650752 | tf_op jit(solution)/shard_map/reduce_scatter | solution.py:253
  305.8 30.8 %copy-start.26 = (f32[1,8192]{1,0:T(1,128)}, f32[1,8192]{1,0:T(1,128)S(1)}, u32[]{:S(2)}) copy-start(f32[1,8192]{1,0:T(1,128)S(1)} %convert_element_type.405) | copy-start | bytes 98308
  309.4 27.2 %copy-start.33 = (f32[128]{0:T(128)}, f32[128]{0:T(128)S(1)}, u32[]{:S(2)}) copy-start(f32[128]{0:T(128)S(1)} %add_sqrt_fusion) | copy-start | bytes 1540
  309.7 33.4 %copy-start.21 = (f32[128,64]{0,1:T(8,128)}, f32[128,64]{0,1:T(8,128)S(1)}, u32[]{:S(2)}) copy-start(f32[128,64]{0,1:T(8,128)S(1)} %get-tuple-element.56) | copy-start | bytes 98308
  309.7 33.4 %copy-start.23 = (f32[128,64]{0,1:T(8,128)}, f32[128,64]{0,1:T(8,128)S(1)}, u32[]{:S(2)}) copy-start(f32[128,64]{0,1:T(8,128)S(1)} %get-tuple-element.57) | copy-start | bytes 98308
  315.7 58.7 %copy-start.20 = (bf16[128,4,128,1]{0,2,3,1:T(8,128)(2,1)}, bf16[128,4,128,1]{0,2,3,1:T(8,128)(2,1)S(1)}, u32[]{:S(2)}) copy-start(bf16[128,4,128,1]{0,2,3,1:T(8,128)(2,1)S(1)} %copy.249) | copy-start | bytes 393220
  343.1 23.1 %collective-permute-start.3 = (bf16[2,128,4,128]{1,3,2,0:T(8,128)(2,1)S(1)}, bf16[2,128,4,128]{1,3,2,0:T(8,128)(2,1)S(1)}, u32[]{:S(2)}, u32[]{:S(2)}) collective-permute-start(bf16[2,128,4,128]{1,3,2,0:T(8,128)(2,1)S(1)} %pad_maximum_fusion), channel_id=1, source_target_pairs={{0,1},{1,2},{2,3},{3,4},{4,5},{5,6},{6,7},{7,8},{8,9},{9,10},{10,1... | collective-permute-start | bytes 786440 | tf_op jit(solution)/shard_map/ppermute | solution.py:21
  344.5 21.1 %collective-permute-start.2 = (bf16[2,128,4,128]{1,3,2,0:T(8,128)(2,1)S(1)}, bf16[2,128,4,128]{1,3,2,0:T(8,128)(2,1)S(1)}, u32[]{:S(2)}, u32[]{:S(2)}) collective-permute-start(bf16[2,128,4,128]{1,3,2,0:T(8,128)(2,1)S(1)} %pad_maximum_fusion), channel_id=1, source_target_pairs={{0,2},{1,3},{2,4},{3,5},{4,6},{5,7},{6,8},{7,9},{8,10},{9,11},{10,... | collective-permute-start | bytes 786440 | tf_op jit(solution)/shard_map/ppermute | solution.py:21
  345.8 19.1 %collective-permute-start.1 = (bf16[2,128,4,128]{1,3,2,0:T(8,128)(2,1)S(1)}, bf16[2,128,4,128]{1,3,2,0:T(8,128)(2,1)S(1)}, u32[]{:S(2)}, u32[]{:S(2)}) collective-permute-start(bf16[2,128,4,128]{1,3,2,0:T(8,128)(2,1)S(1)} %pad_maximum_fusion), channel_id=1, source_target_pairs={{0,3},{1,4},{2,5},{3,6},{4,7},{5,8},{6,9},{7,10},{8,11},{9,12},{10... | collective-permute-start | bytes 786440 | tf_op jit(solution)/shard_map/ppermute | solution.py:21
  347.1 17.1 %collective-permute-start = (bf16[2,128,4,128]{1,3,2,0:T(8,128)(2,1)S(1)}, bf16[2,128,4,128]{1,3,2,0:T(8,128)(2,1)S(1)}, u32[]{:S(2)}, u32[]{:S(2)}) collective-permute-start(bf16[2,128,4,128]{1,3,2,0:T(8,128)(2,1)S(1)} %pad_maximum_fusion), channel_id=1, source_target_pairs={{0,4},{1,5},{2,6},{3,7},{4,8},{5,9},{6,10},{7,11},{8,12},{9,13},{1... | collective-permute-start | bytes 786440 | tf_op jit(solution)/shard_map/ppermute | solution.py:21
  356.4 13.9 %copy-start = (f32[4,8,128,128]{2,3,1,0:T(8,128)}, f32[4,8,128,128]{2,3,1,0:T(8,128)S(1)}, u32[]{:S(2)}) copy-start(f32[4,8,128,128]{2,3,1,0:T(8,128)S(1)} %get-tuple-element.59) | copy-start | bytes 6291460
  364.2 13.0 %copy-start.16 = (bf16[2,128,4,128]{1,3,2,0:T(8,128)(2,1)}, bf16[2,128,4,128]{1,3,2,0:T(8,128)(2,1)S(1)}, u32[]{:S(2)}) copy-start(bf16[2,128,4,128]{1,3,2,0:T(8,128)(2,1)S(1)} %collective-permute-done) | copy-start | bytes 786436
  364.9 13.6 %copy-start.14 = (bf16[2,128,4,128]{1,3,2,0:T(8,128)(2,1)}, bf16[2,128,4,128]{1,3,2,0:T(8,128)(2,1)S(1)}, u32[]{:S(2)}) copy-start(bf16[2,128,4,128]{1,3,2,0:T(8,128)(2,1)S(1)} %collective-permute-done.1) | copy-start | bytes 786436
  366.3 15.0 %copy-start.18 = (bf16[2,128,4,128]{1,3,2,0:T(8,128)(2,1)}, bf16[2,128,4,128]{1,3,2,0:T(8,128)(2,1)S(1)}, u32[]{:S(2)}) copy-start(bf16[2,128,4,128]{1,3,2,0:T(8,128)(2,1)S(1)} %collective-permute-done.3) | copy-start | bytes 786436
  370.3 10.9 %copy-start.30 = (f32[4,8,128]{2,1,0:T(8,128)}, f32[4,8,128]{2,1,0:T(8,128)S(1)}, u32[]{:S(2)}) copy-start(f32[4,8,128]{2,1,0:T(8,128)S(1)} %add_add_fusion) | copy-start | bytes 49156
  382.7 20.8 %copy-start.1 = (bf16[1,128,8192]{2,1,0:T(8,128)(2,1)S(1)}, bf16[1,128,8192]{2,1,0:T(8,128)(2,1)}, u32[]{:S(2)}) copy-start(bf16[1,128,8192]{2,1,0:T(8,128)(2,1)} %param.9) | copy-start | bytes 6291460
  382.7 20.8 %copy-start.27 = (f32[1,8192]{1,0:T(1,128)S(1)}, f32[1,8192]{1,0:T(1,128)}, u32[]{:S(2)}) copy-start(f32[1,8192]{1,0:T(1,128)} %copy-done.26) | copy-start | bytes 98308
  382.7 20.8 %copy-start.34 = (f32[128]{0:T(128)S(1)}, f32[128]{0:T(128)}, u32[]{:S(2)}) copy-start(f32[128]{0:T(128)} %copy-done.33) | copy-start | bytes 1540
  382.7 10.2 %collective-permute-start.4 = (bf16[2,128,4,128]{1,3,2,0:T(8,128)(2,1)S(1)}, bf16[2,128,4,128]{1,3,2,0:T(8,128)(2,1)S(1)}, u32[]{:S(2)}, u32[]{:S(2)}) collective-permute-start(bf16[2,128,4,128]{1,3,2,0:T(8,128)(2,1)S(1)} %pad_maximum_fusion.1), channel_id=1, source_target_pairs={{1,0},{2,1},{3,2},{4,3},{5,4},{6,5},{7,6},{8,7},{9,8},{10,9},{11,1... | collective-permute-start | bytes 786440 | tf_op jit(solution)/shard_map/ppermute | solution.py:21
  384.2 18.2 %collective-permute-start.5 = (bf16[2,128,4,128]{1,3,2,0:T(8,128)(2,1)S(1)}, bf16[2,128,4,128]{1,3,2,0:T(8,128)(2,1)S(1)}, u32[]{:S(2)}, u32[]{:S(2)}) collective-permute-start(bf16[2,128,4,128]{1,3,2,0:T(8,128)(2,1)S(1)} %pad_maximum_fusion.2), channel_id=1, source_target_pairs={{2,0},{3,1},{4,2},{5,3},{6,4},{7,5},{8,6},{9,7},{10,8},{11,9},{12,... | collective-permute-start | bytes 786440 | tf_op jit(solution)/shard_map/ppermute | solution.py:21
  385.5 16.9 %collective-permute-start.6 = (bf16[2,128,4,128]{1,3,2,0:T(8,128)(2,1)S(1)}, bf16[2,128,4,128]{1,3,2,0:T(8,128)(2,1)S(1)}, u32[]{:S(2)}, u32[]{:S(2)}) collective-permute-start(bf16[2,128,4,128]{1,3,2,0:T(8,128)(2,1)S(1)} %pad_maximum_fusion.3), channel_id=1, source_target_pairs={{3,0},{4,1},{5,2},{6,3},{7,4},{8,5},{9,6},{10,7},{11,8},{12,9},{13... | collective-permute-start | bytes 786440 | tf_op jit(solution)/shard_map/ppermute | solution.py:21
  386.8 15.5 %collective-permute-start.7 = (bf16[2,128,4,128]{1,3,2,0:T(8,128)(2,1)S(1)}, bf16[2,128,4,128]{1,3,2,0:T(8,128)(2,1)S(1)}, u32[]{:S(2)}, u32[]{:S(2)}) collective-permute-start(bf16[2,128,4,128]{1,3,2,0:T(8,128)(2,1)S(1)} %pad_maximum_fusion.4), channel_id=1, source_target_pairs={{4,0},{5,1},{6,2},{7,3},{8,4},{9,5},{10,6},{11,7},{12,8},{13,9},{1... | collective-permute-start | bytes 786440 | tf_op jit(solution)/shard_map/ppermute | solution.py:21
  392.9 9.9 %copy-start.38 = (bf16[2,128,4,128]{1,3,2,0:T(8,128)(2,1)}, bf16[2,128,4,128]{1,3,2,0:T(8,128)(2,1)S(1)}, u32[]{:S(2)}) copy-start(bf16[2,128,4,128]{1,3,2,0:T(8,128)(2,1)S(1)} %collective-permute-done.4) | copy-start | bytes 786436
  409.2 474.6 %reduce-scatter.3.cloned.1.call-start = ((), (), s32[]{:S(2)}) async-start(), calls=%async_computation.4 | async-start | bytes 8650752 | tf_op jit(solution)/shard_map/reduce_scatter | solution.py:250
  434.8 6.2 collective-permute-start.8
  445.9 72.2 %collective-permute-start.9 = (bf16[128,8192]{1,0:T(8,128)(2,1)}, bf16[128,8192]{1,0:T(8,128)(2,1)}, u32[]{:S(2)}, u32[]{:S(2)}) collective-permute-start(bf16[128,8192]{1,0:T(8,128)(2,1)} %fusion.6), channel_id=1, source_target_pairs={{32,0},{64,32},{96,64},{33,1},{65,33},{97,65},{34,2},{66,34},{98,6... | collective-permute-start | bytes 6291464 | tf_op jit(solution)/shard_map/ppermute | solution.py:21
  524.2 183.5 %collective-permute-start.10 = (bf16[128,8192]{1,0:T(8,128)(2,1)}, bf16[128,8192]{1,0:T(8,128)(2,1)}, u32[]{:S(2)}, u32[]{:S(2)}) collective-permute-start(bf16[128,8192]{1,0:T(8,128)(2,1)} %fusion.7), channel_id=1, source_target_pairs={{32,0},{64,32},{96,64},{33,1},{65,33},{97,65},{34,2},{66,34},{98,6... | collective-permute-start | bytes 6291464 | tf_op jit(solution)/shard_map/ppermute | solution.py:21
  (31 other events, 84.9 us)
Sparse Core Ops, SparseCore 0:
  10.2 314.8 all-gather.2
  409.3 213.8 reduce-scatter.4
  625.7 258.0 reduce-scatter.2
